TPU v7x, 32 devices: a whole 2x2x4 slice. The times are simulated.
32 devices in a mesh: chan: 4 (over x, core), az: 2 (over y), rng: 4 (over z).
Axes of the slice: x: 2, y: 2, z: 4, core: 2. Of those that a mesh axis runs over, the one named last changes fastest.
Arguments:
- raw: float32 [2, 16, 64, 16384], P(None, 'chan', 'rng', 'az'), may hold values from -6 to 6
- taps: float32 [2, 17, 64], P(None, None, 'rng'), may hold values from -1.5 to 1.5
- recon: float32 [2, 16, 16, 16384], P(None, 'az', None, ('chan', 'rng')), may hold values from -1 to 1
- channel_slot: int32 [16], replicated, may hold values from 0 to 15, each once
Outputs:
- reconstructed: float32 [2, 16, 4, 16, 16384], P(None, None, None, 'az', ('chan', 'rng'))
Inputs may be any that keep to these rules, and one draw needn't show every extreme that they name: `channel_slot`: a permutation of the channels.
All inputs are finite; a program needn't handle non-finite values.
Results may differ from a plain program's by a relative error of at most 0.0003.
Values sent between devices are 32-bit elements; how exact they have to be, the bound alone decides.
No kernel may reach another device: no remote copies, remote signals or barrier semaphores. Data moves between devices by JAX's collectives and lax.ppermute only.
A program may use at most 192 MiB of HBM per device.

v0:
```python
import math
import jax
import jax.numpy as jnp
from jax import lax
from jax.sharding import PartitionSpec as P


def with_halo(shard, sides, width):
    for axis, dim in sides:
        size, length = (lax.axis_size(axis), shard.shape[dim])
        up = [(i, (i + 1) % size) for i in range(size - 1)]
        down = [(j, i) for i, j in up]
        last = lax.slice_in_dim(shard, length - width, length, axis=dim)
        leading = lax.slice_in_dim(shard, 0, width, axis=dim)
        before = lax.ppermute(last, axis, up)
        after = lax.ppermute(leading, axis, down)
        shard = jnp.concatenate([before, shard, after], axis=dim)
    return shard


def phases(first, second, length):
    left = jnp.arange(first, dtype=jnp.int32)
    right = jnp.arange(second, dtype=jnp.int32)
    product = left[:, None] * right[None, :] % length
    angle = product.astype(jnp.float32) * (2.0 * math.pi / length)
    return (jnp.cos(angle), jnp.sin(angle))


def azimuth_fft(block):
    count = block.shape[-1]
    rows = math.isqrt(count)
    while count % rows:
        rows = rows - 1
    cols = count // rows
    lead = block.shape[1:-1]
    high = lax.Precision.HIGHEST
    real_in = block[0].reshape(lead + (rows, cols))
    imag_in = block[1].reshape(lead + (rows, cols))
    cosine_first, sine_first = phases(rows, rows, rows)
    first_real = jnp.einsum("...ab,af->...bf", real_in, cosine_first, precision=high) + jnp.einsum(
        "...ab,af->...bf", imag_in, sine_first, precision=high
    )
    first_imag = jnp.einsum("...ab,af->...bf", imag_in, cosine_first, precision=high) - jnp.einsum(
        "...ab,af->...bf", real_in, sine_first, precision=high
    )
    twist_cos, twist_sin = phases(cols, rows, count)
    turned_real = first_real * twist_cos + first_imag * twist_sin
    turned_imag = first_imag * twist_cos - first_real * twist_sin
    cosine_second, sine_second = phases(cols, cols, cols)
    out_real = jnp.einsum(
        "...bf,bg->...gf", turned_real, cosine_second, precision=high
    ) + jnp.einsum("...bf,bg->...gf", turned_imag, sine_second, precision=high)
    out_imag = jnp.einsum(
        "...bf,bg->...gf", turned_imag, cosine_second, precision=high
    ) - jnp.einsum("...bf,bg->...gf", turned_real, sine_second, precision=high)
    scale = 1.0 / math.sqrt(count)
    return jnp.stack([out_real.reshape(lead + (count,)), out_imag.reshape(lead + (count,))]) * scale


def shards(raw, taps, recon, channel_slot):
    width = taps.shape[1]
    half = (width - 1) // 2
    strip_rows = raw.shape[2]
    padded = with_halo(raw, (("rng", 2),), half)
    real_part = jnp.zeros(raw.shape[1:], jnp.float32)
    imag_part = jnp.zeros(raw.shape[1:], jnp.float32)
    for offset in range(width):
        seg_real = padded[0, :, offset : offset + strip_rows, :]
        seg_imag = padded[1, :, offset : offset + strip_rows, :]
        tap_real = taps[0, offset][None, :, None]
        tap_imag = taps[1, offset][None, :, None]
        real_part = real_part + tap_real * seg_real - tap_imag * seg_imag
        imag_part = imag_part + tap_real * seg_imag + tap_imag * seg_real
    filtered = jnp.stack([real_part, imag_part])
    spectrum = azimuth_fft(lax.all_to_all(filtered, "az", split_axis=2, concat_axis=3, tiled=True))
    strips = lax.axis_size("rng")
    groups = lax.axis_size("chan")
    local_channels = spectrum.shape[1]
    local_range = spectrum.shape[2]
    moved = lax.all_to_all(
        spectrum[:, None], ("chan", "rng"), split_axis=4, concat_axis=1, tiled=True
    )
    bins = moved.shape[-1]
    moved = moved.reshape((2, groups, strips, local_channels, local_range, bins))
    doppler = jnp.transpose(moved, (0, 1, 3, 2, 4, 5)).reshape(
        (2, groups * local_channels, strips * local_range, bins)
    )
    channels = doppler.shape[1]
    selector = (channel_slot[:, None] == jnp.arange(channels, dtype=jnp.int32)[None, :]).astype(
        jnp.float32
    )
    piece = lax.all_gather(recon, "az", axis=1, tiled=True)
    arranged = jnp.einsum("pkjf,cj->pkcf", piece, selector, precision=lax.Precision.HIGHEST)
    shape = (piece.shape[1], doppler.shape[2], doppler.shape[3])
    out_real = jnp.zeros(shape, jnp.float32)
    out_imag = jnp.zeros(shape, jnp.float32)
    for channel in range(channels):
        mat_real = arranged[0, :, channel, None, :]
        mat_imag = arranged[1, :, channel, None, :]
        data_real = doppler[0, channel][None]
        data_imag = doppler[1, channel][None]
        out_real = out_real + mat_real * data_real - mat_imag * data_imag
        out_imag = out_imag + mat_real * data_imag + mat_imag * data_real
    result = jnp.stack([out_real, out_imag])
    total_range = result.shape[2]
    return result.reshape((2, result.shape[1], strips, total_range // strips, result.shape[3]))


def solution(mesh):
    return jax.shard_map(
        shards,
        mesh=mesh,
        in_specs=(
            P(None, "chan", "rng", "az"),
            P(None, None, "rng"),
            P(None, "az", None, ("chan", "rng")),
            P(),
        ),
        out_specs=P(None, None, None, "az", ("chan", "rng")),
        check_vma=False,
    )
```

profile of v0, /device:TPU:0, one launch (start us, length us, event | category | flops | bytes accessed | tf_op | source)
XLA Modules:
  0.0 701.0 jit_solution(1237962557530691339)
XLA Ops:
  6.5 2.5 fusion.71
  9.0 5.1 collective-permute-start
  14.1 1.3 collective-permute-start.1
  15.5 0.5 slice_reduce_fusion.33
  15.9 0.4 slice_reduce_fusion.32
  16.4 42.5 %collective-permute-done = f32[2,4,8,8192]{3,2,1,0:T(8,128)S(1)} collective-permute-done((f32[2,4,8,8192]{3,2,1,0:T(8,128)S(1)}, f32[2,4,8,8192]{3,2,1,0:T(8,128)S(1)}, u32[]{:S(2)}, u32[]{:S(2)}) %collective-permute-start) | collective-permute-done | bytes 2097184 | tf_op jit(solution)/shard_map/ppermute | solution.py:15
  58.9 1.5 constant_dynamic-update-slice_fusion.1
  60.4 4.2 constant_dynamic-update-slice_fusion
  64.6 1.5 constant_dynamic-update-slice_fusion.2
  66.1 44.7 %multiply_subtract_fusion.2 = f32[1,4,16,8192]{3,2,1,0:T(8,128)} fusion(f32[2,4,24,8192]{3,2,1,0:T(8,128)} %constant_dynamic-update-slice_fusion.2, f32[2,4,24,8192]{3,2,1,0:T(8,128)} %get-tuple-element.73, f32[2,4,16,8192]{3,2,1,0:T(8,128)S(1)} %copy-done, f32[16]{0:T(128)S(1)} %get-tuple-element.37, f32[16]{0:T(128)S(1)} %get-tuple-element.38, ...), kind=kLoop, calls=%fused_computation.11 | loop fusion | flops 35127296 | bytes 73402496 | tf_op jit(solution)/shard_map/sub | solution.py:72
  110.8 44.8 %multiply_add_fusion.2 = f32[1,4,16,8192]{3,2,1,0:T(8,128)} fusion(f32[2,4,24,8192]{3,2,1,0:T(8,128)} %constant_dynamic-update-slice_fusion.2, f32[2,4,24,8192]{3,2,1,0:T(8,128)} %get-tuple-element.73, f32[2,4,16,8192]{3,2,1,0:T(8,128)S(1)} %copy-done, f32[16]{0:T(128)S(1)} %get-tuple-element.37, f32[16]{0:T(128)S(1)} %get-tuple-element.38, ...), kind=kLoop, calls=%fused_computation.10 | loop fusion | flops 35127296 | bytes 73402496 | tf_op jit(solution)/shard_map/add | solution.py:73
  155.5 2.5 pad_maximum_fusion
  158.1 4.7 copy.126
  162.8 5.8 all-to-all-start
  168.9 0.3 fusion.23
  169.3 46.1 %all-to-all-done = f32[2,4,16,8192]{3,1,0,2:T(4,128)} async-done(((f32[2,4,16,8192]{3,1,0,2:T(4,128)}), f32[2,4,16,8192]{3,1,0,2:T(4,128)}, u32[]{:S(2)}, u32[]{:S(2)}) %all-to-all-start) | async-done | bytes 4194336 | tf_op jit(solution)/shard_map/all_to_all | solution.py:75
  215.4 5.4 copy.224
  220.8 2.3 fusion.70
  223.1 3.1 reshape_squeeze.7
  226.1 4.9 fusion.6
  231.0 4.2 reshape_squeeze.6
  235.2 5.4 fusion.8
  240.6 3.7 convolution_subtract_fusion
  244.3 3.6 convolution_add_fusion
  247.9 2.7 fusion
  250.6 3.5 fusion.1
  254.1 3.7 add_bitcast_fusion
  257.8 2.7 stack.18
  260.5 5.8 subtract_bitcast_fusion
  266.3 2.9 stack.19
  269.2 3.9 maximum_multiply_fusion
  273.1 44.6 %copy.138 = f32[2,1,4,8,16384]{3,2,1,0,4:T(4,128)} copy(f32[2,1,4,8,16384]{4,3,2,1,0:T(8,128)} %maximum_multiply_fusion) | data formatting | bytes 8388608 | tf_op jit(solution)/shard_map/mul | solution.py:57
  317.7 82.5 %reshape.729 = f32[16,1,65536]{2,1,0:T(1,128)} reshape(f32[16384,2,1,4,8]{4,3,2,1,0:T(4,128)} %bitcast.180) | data formatting | bytes 8388608
  400.3 7.0 all-to-all-start.1
  407.3 0.7 all-gather.2.cloned.1.call-update
  408.0 35.1 %all-gather.2.cloned.1.call-done = f32[2,16,16,1024]{3,2,1,0:T(8,128)} async-done(((f32[2,8,16,1024]{3,2,1,0:T(8,128)}), f32[2,16,16,1024]{3,2,1,0:T(8,128)}) %all-gather.2.cloned.1.call-update) | async-done | bytes 2097168 | tf_op jit(solution)/shard_map/all_gather | solution.py:92
  443.1 2.7 convolution_bitcast_fusion
  445.8 1.1 fusion.72
  447.2 0.8 fusion.73
  448.2 53.3 %all-to-all-done.1 = f32[16,1,65536]{2,1,0:T(1,128)} async-done(((f32[16,1,65536]{2,1,0:T(1,128)}), f32[16,1,65536]{2,1,0:T(1,128)}, u32[]{:S(2)}, u32[]{:S(2)}) %all-to-all-start.1) | async-done | bytes 4194336 | tf_op jit(solution)/shard_map/all_to_all | solution.py:80
  501.6 0.5 broadcast.1262
  502.1 13.7 %reduce.68 = f32[16,65536]{1,0:T(8,128)} reduce(f32[16,1,65536]{2,1,0:T(1,128)} %all-to-all-done.1, f32[]{:T(128)} %broadcast.1262), dimensions={1}, to_apply=%all_to_all.25.reduce_sub_computation | reduce | bytes 8388612 | tf_op jit(solution)/shard_map/all_to_all | solution.py:80
  515.8 109.0 %reshape.730 = f32[16384,2,1,4,8]{4,3,2,1,0:T(4,128)} reshape(f32[16,65536]{1,0:T(8,128)} %reduce.68) | data formatting | bytes 8388608
  624.8 53.3 %copy.158 = f32[2,1,4,8,16,1024]{5,3,2,4,0,1:T(8,128)} copy(f32[2,1,4,8,16,1024]{3,2,0,5,4,1:T(4,128)} %bitcast.17) | data formatting | bytes 8388608 | tf_op jit(solution)/shard_map/all_to_all | solution.py:80
  678.1 2.5 copy.141
  681.0 5.3 multiply_subtract_fusion
  686.3 5.3 multiply_add_fusion
  691.7 2.3 pad_maximum_fusion.1
  (41 shorter events, 1.3 us)
Async XLA Ops:
  6.5 8.9 %copy-start.7 = (f32[2,17,16]{1,2,0:T(8,128)S(1)}, f32[2,17,16]{1,2,0:T(8,128)}, u32[]{:S(2)}) copy-start(f32[2,17,16]{1,2,0:T(8,128)} %param.5) | copy-start | bytes 6532
  9.0 49.8 %collective-permute-start = (f32[2,4,8,8192]{3,2,1,0:T(8,128)S(1)}, f32[2,4,8,8192]{3,2,1,0:T(8,128)S(1)}, u32[]{:S(2)}, u32[]{:S(2)}) collective-permute-start(f32[2,4,8,8192]{3,2,1,0:T(8,128)S(1)} %get-tuple-element.75), channel_id=1, source_target_pairs={{0,1},{1,2},{2,3},{4,5},{5,6},{6,7},{8,9},{9,10},{10,11},{12,13},{... | collective-permute-start | bytes 6291464 | tf_op jit(solution)/shard_map/ppermute | solution.py:15
  14.1 50.5 %collective-permute-start.1 = (f32[2,4,8,8192]{3,2,1,0:T(8,128)S(1)}, f32[2,4,8,8192]{3,2,1,0:T(8,128)S(1)}, u32[]{:S(2)}, u32[]{:S(2)}) collective-permute-start(f32[2,4,8,8192]{3,2,1,0:T(8,128)S(1)} %get-tuple-element.76), channel_id=1, source_target_pairs={{1,0},{2,1},{3,2},{5,4},{6,5},{7,6},{9,8},{10,9},{11,10},{13,12},{... | collective-permute-start | bytes 6291464 | tf_op jit(solution)/shard_map/ppermute | solution.py:16
  16.4 44.0 %copy-start = (f32[2,4,16,8192]{3,2,1,0:T(8,128)S(1)}, f32[2,4,16,8192]{3,2,1,0:T(8,128)}, u32[]{:S(2)}) copy-start(f32[2,4,16,8192]{3,2,1,0:T(8,128)} %param.4) | copy-start | bytes 12582916
  162.8 52.6 %all-to-all-start = ((f32[2,4,16,8192]{3,1,0,2:T(4,128)}), f32[2,4,16,8192]{3,1,0,2:T(4,128)}, u32[]{:S(2)}, u32[]{:S(2)}) async-start(f32[2,4,16,8192]{3,1,0,2:T(4,128)} %copy.126), calls=%async_computation | async-start | bytes 8388608 | tf_op jit(solution)/shard_map/all_to_all | solution.py:75
  226.1 4.9 copy-start.2
  235.2 5.4 copy-start.4
  235.2 5.4 copy-start.5
  240.6 3.7 copy-start.3
  247.9 6.2 copy-start.1
  266.3 2.9 copy-start.6
  400.3 42.8 %copy-start.8 = (s32[16]{0:T(128)S(1)}, s32[16]{0:T(128)}, u32[]{:S(2)}) copy-start(s32[16]{0:T(128)} %param.7) | copy-start | bytes 196
  400.3 101.3 %all-to-all-start.1 = ((f32[16,1,65536]{2,1,0:T(1,128)}), f32[16,1,65536]{2,1,0:T(1,128)}, u32[]{:S(2)}, u32[]{:S(2)}) async-start(f32[16,1,65536]{2,1,0:T(1,128)} %reshape.729), calls=%async_computation.1 | async-start | bytes 8388608 | tf_op jit(solution)/shard_map/all_to_all | solution.py:80
  407.3 35.8 %all-gather.2.cloned.1.call-start = ((), (), s32[]{:S(2)}) async-start(), calls=%async_computation.2 | async-start | bytes 3145728 | tf_op jit(solution)/shard_map/all_gather | solution.py:92
Sparse Core Ops, SparseCore 0:
  409.6 33.4 all-gather.1
where the time goes:
time: 714 us; the launch traced here: 701 us
  local copies, waits for them, and re-layouts  331 us (46%)
  waiting for transfers between devices  178 us (25%)
  other arithmetic  123 us (17%)
  matrix products  35.9 us (5%)
  starting transfers between devices  19.2 us (3%)
  between operations  14 us (2%)
    unnamed x37, local copies, waits for them, and re-layouts  193 us
    all_to_all x2, local copies, waits for them, and re-layouts, shards(): lax.all_to_all(spectrum[:, None], ('chan', 'rng'), split_axis=4, concat_a...  53.9 us
    all_to_all x1, waiting for transfers between devices, shards(): lax.all_to_all(spectrum[:, None], ('chan', 'rng'), split_axis=4, concat_a...  53.3 us
    all_to_all x1, waiting for transfers between devices, shards(): lax.all_to_all(filtered, 'az', split_axis=2, concat_axis=3, tiled=True)  46.1 us
    add x1, other arithmetic, shards(): imag_part = imag_part + tap_real * seg_imag + tap_imag * seg_real  44.8 us
    sub x1, other arithmetic, shards(): real_part = real_part + tap_real * seg_real - tap_imag * seg_imag  44.7 us
    mul x1, local copies, waits for them, and re-layouts, azimuth_fft(): jnp.stack([out_real.reshape(lead + (count,)), out_imag.reshape(lead + (co...  44.6 us
    ppermute x1, waiting for transfers between devices, with_halo(): before = lax.ppermute(last, axis, up)  42.5 us
  transfers between devices with their start and end apart: 5, of which 4 were waited for; matrix products, arithmetic and copies ran while one was open for 2% of the time, Pallas kernels for 0%

commit v1 on v0

--- a/solution.py
+++ b/solution.py
@@ -3,6 +3,29 @@
 import jax.numpy as jnp
 from jax import lax
 from jax.sharding import PartitionSpec as P
+
+
+def cut_along(x, dim, size):
+    before, after = (x.shape[:dim], x.shape[dim + 1 :])
+    return jnp.moveaxis(x.reshape(*before, size, -1, *after), dim, 0)
+
+
+def laid_out(blocks, dim):
+    lengths = list(blocks.shape[1:])
+    lengths[dim] *= blocks.shape[0]
+    return jnp.moveaxis(blocks, 0, dim).reshape(lengths)
+
+
+def sent_to_each(x, axis, split_dim, concat_dim):
+    peers, index = (lax.axis_size(axis), lax.axis_index(axis))
+    pieces = cut_along(x, split_dim, peers)
+    filled = pieces
+    for lap in range(1, peers):
+        target, source = ((index + lap) % peers, (index - lap) % peers)
+        sent = lax.dynamic_index_in_dim(pieces, target, 0)
+        other = lax.ppermute(sent, axis, [(i, (i + lap) % peers) for i in range(peers)])
+        filled = lax.dynamic_update_slice_in_dim(filled, other, source, axis=0)
+    return laid_out(filled, concat_dim)
 
 
 def with_halo(shard, sides, width):
@@ -77,9 +100,7 @@
     groups = lax.axis_size("chan")
     local_channels = spectrum.shape[1]
     local_range = spectrum.shape[2]
-    moved = lax.all_to_all(
-        spectrum[:, None], ("chan", "rng"), split_axis=4, concat_axis=1, tiled=True
-    )
+    moved = sent_to_each(spectrum[:, None], ("chan", "rng"), 4, 1)
     bins = moved.shape[-1]
     moved = moved.reshape((2, groups, strips, local_channels, local_range, bins))
     doppler = jnp.transpose(moved, (0, 1, 3, 2, 4, 5)).reshape(

time: 714 us -> 399 us (0.56); the launches traced: 701 us -> 395 us
  local copies, waits for them, and re-layouts: 331 us -> 55.6 us
  waiting for transfers between devices: 178 us -> 134 us
  starting transfers between devices: 19.2 us -> 49.4 us
  other arithmetic: 123 us -> 107 us
    unnamed x37 -> x65, local copies, waits for them, and re-layouts: 193 us -> 9.28 us
    ppermute x0 -> x15, waiting for transfers between devices: none -> 56.2 us  [sent_to_each(): lax.ppermute(sent, axis, [(i, (i + lap) % peers) for i in range(peers)])]
    all_to_all x2 -> x0, local copies, waits for them, and re-layouts: 53.9 us -> none  [shards(): lax.all_to_all(spectrum[:, None], ('chan', 'rng'), split_axis=4, concat_a...]
    all_to_all x1 -> x0, waiting for transfers between devices: 53.3 us -> none  [shards(): lax.all_to_all(spectrum[:, None], ('chan', 'rng'), split_axis=4, concat_a...]
    mul x1 -> x0, local copies, waits for them, and re-layouts: 44.6 us -> none  [azimuth_fft(): jnp.stack([out_real.reshape(lead + (count,)), out_imag.reshape(lead + (co...]
    ppermute x0 -> x15, starting transfers between devices: none -> 35.9 us  [sent_to_each(): lax.ppermute(sent, axis, [(i, (i + lap) % peers) for i in range(peers)])]
    all_gather x1, waiting for transfers between devices: 35.1 us -> 0.02 us  [shards(): piece = lax.all_gather(recon, 'az', axis=1, tiled=True)]
    all_to_all x1 -> x0, other arithmetic: 13.7 us -> none  [shards(): lax.all_to_all(spectrum[:, None], ('chan', 'rng'), split_axis=4, concat_a...]
  transfers between devices with their start and end apart: 5 -> 19, of which waited for: 4 -> 8; matrix products, arithmetic and copies ran while one was open for 2% -> 30% of each run, Pallas kernels for 0% -> 0%
where the time goes in v1:
time: 399 us; the launch traced here: 395 us
  waiting for transfers between devices  134 us (34%)
  other arithmetic  107 us (27%)
  local copies, waits for them, and re-layouts  55.6 us (14%)
  starting transfers between devices  49.4 us (12%)
  matrix products  33.6 us (8%)
  between operations  14.9 us (4%)
    ppermute x15, waiting for transfers between devices, sent_to_each(): lax.ppermute(sent, axis, [(i, (i + lap) % peers) for i in range(peers)])  56.2 us
    add x1, other arithmetic, shards(): imag_part = imag_part + tap_real * seg_imag + tap_imag * seg_real  44.9 us
    sub x1, other arithmetic, shards(): real_part = real_part + tap_real * seg_real - tap_imag * seg_imag  44.8 us
    ppermute x1, waiting for transfers between devices, with_halo(): before = lax.ppermute(last, axis, up)  40.2 us
    all_to_all x1, waiting for transfers between devices, shards(): lax.all_to_all(filtered, 'az', split_axis=2, concat_axis=3, tiled=True)  37.6 us
    ppermute x15, starting transfers between devices, sent_to_each(): lax.ppermute(sent, axis, [(i, (i + lap) % peers) for i in range(peers)])  35.9 us
    another operation x4, local copies, waits for them, and re-layouts, azimuth_fft(): jnp.stack([out_real.reshape(lead + (count,)), out_imag.reshape(lead + (co...  10.1 us
    unnamed x65, local copies, waits for them, and re-layouts  9.28 us
  transfers between devices with their start and end apart: 19, of which 8 were waited for; matrix products, arithmetic and copies ran while one was open for 30% of the time, Pallas kernels for 0%

profile of v1, /device:TPU:0, one launch (start us, length us, event | category | flops | bytes accessed | tf_op | source)
XLA Modules:
  0.0 394.5 jit_solution(16569184598536407608)
XLA Ops:
  6.5 4.7 %fusion.72 = (f32[2,4,8,8192]{3,2,1,0:T(8,128)}, f32[2,4,8,8192]{3,2,1,0:T(8,128)}) fusion(f32[2,4,16,8192]{3,2,1,0:T(8,128)} %param.4), kind=kLoop, calls=%fused_computation.217 | loop fusion | bytes 8388608 | tf_op jit(solution)/shard_map/slice | solution.py:36
  11.2 6.3 %collective-permute-start = (f32[2,4,8,8192]{3,2,1,0:T(8,128)}, f32[2,4,8,8192]{3,2,1,0:T(8,128)}, u32[]{:S(2)}, u32[]{:S(2)}) collective-permute-start(f32[2,4,8,8192]{3,2,1,0:T(8,128)} %get-tuple-element.92), channel_id=1, source_target_pairs={{0,1},{1,2},{2,3},{4,5},{5,6},{6,7},{8,9},{9,10},{10,11},{12,13},{... | collective-permute-start | bytes 6291464 | tf_op jit(solution)/shard_map/ppermute | solution.py:38
  17.5 1.3 collective-permute-start.1
  21.1 40.2 %collective-permute-done = f32[2,4,8,8192]{3,2,1,0:T(8,128)} collective-permute-done((f32[2,4,8,8192]{3,2,1,0:T(8,128)}, f32[2,4,8,8192]{3,2,1,0:T(8,128)}, u32[]{:S(2)}, u32[]{:S(2)}) %collective-permute-start) | collective-permute-done | bytes 2097184 | tf_op jit(solution)/shard_map/ppermute | solution.py:38
  61.3 3.1 constant_dynamic-update-slice_fusion.1
  64.4 4.2 %constant_dynamic-update-slice_fusion = (f32[2,4,24,8192]{3,2,1,0:T(8,128)}, f32[2,4,24,8192]{3,2,1,0:T(8,128)}) fusion(f32[2,4,24,8192]{3,2,1,0:T(8,128)} %constant_dynamic-update-slice_fusion.1, f32[2,4,16,8192]{3,2,1,0:T(8,128)S(1)} %copy-done), kind=kLoop, calls=%fused_computation.127 | loop fusion | bytes 12582912 | tf_op jit(solution)/shard_map/concatenate | solution.py:40
  68.6 3.0 constant_dynamic-update-slice_fusion.2
  71.7 44.9 %multiply_add_fusion.2 = f32[1,4,16,8192]{3,2,1,0:T(8,128)} fusion(f32[2,4,24,8192]{3,2,1,0:T(8,128)} %constant_dynamic-update-slice_fusion.2, f32[2,4,24,8192]{3,2,1,0:T(8,128)} %get-tuple-element.90, f32[2,4,16,8192]{3,2,1,0:T(8,128)S(1)} %copy-done, f32[16]{0:T(128)S(1)} %get-tuple-element.37, f32[16]{0:T(128)S(1)} %get-tuple-element.38, ...), kind=kLoop, calls=%fused_computation.10 | loop fusion | flops 35127296 | bytes 73402496 | tf_op jit(solution)/shard_map/add | solution.py:96
  116.6 44.8 %multiply_subtract_fusion.2 = f32[1,4,16,8192]{3,2,1,0:T(8,128)} fusion(f32[2,4,24,8192]{3,2,1,0:T(8,128)} %constant_dynamic-update-slice_fusion.2, f32[2,4,24,8192]{3,2,1,0:T(8,128)} %get-tuple-element.90, f32[2,4,16,8192]{3,2,1,0:T(8,128)S(1)} %copy-done, f32[16]{0:T(128)S(1)} %get-tuple-element.37, f32[16]{0:T(128)S(1)} %get-tuple-element.38, ...), kind=kLoop, calls=%fused_computation.11 | loop fusion | flops 35127296 | bytes 73402496 | tf_op jit(solution)/shard_map/sub | solution.py:95
  161.4 2.5 pad_maximum_fusion
  163.9 4.7 %copy.76 = f32[2,4,16,8192]{3,1,0,2:T(4,128)} copy(f32[2,4,16,8192]{3,2,1,0:T(8,128)S(1)} %pad_maximum_fusion) | data formatting | bytes 8388608 | tf_op jit(solution)/shard_map/stack | solution.py:97
  168.6 6.0 %all-to-all-start = ((f32[2,4,16,8192]{3,1,0,2:T(4,128)}), f32[2,4,16,8192]{3,1,0,2:T(4,128)}, u32[]{:S(2)}, u32[]{:S(2)}) async-start(f32[2,4,16,8192]{3,1,0,2:T(4,128)} %copy.76), calls=%async_computation | async-start | bytes 8388608 | tf_op jit(solution)/shard_map/all_to_all | solution.py:98
  174.6 2.7 convolution_bitcast_fusion
  177.4 1.5 fusion.73
  179.2 1.3 fusion.74
  183.8 37.6 %all-to-all-done = f32[2,4,16,8192]{3,1,0,2:T(4,128)} async-done(((f32[2,4,16,8192]{3,1,0,2:T(4,128)}), f32[2,4,16,8192]{3,1,0,2:T(4,128)}, u32[]{:S(2)}, u32[]{:S(2)}) %all-to-all-start) | async-done | bytes 4194336 | tf_op jit(solution)/shard_map/all_to_all | solution.py:98
  221.4 5.4 %copy.171 = f32[2,4,2,8,8192]{4,2,3,1,0:T(2,128)S(1)} copy(f32[2,4,2,8,8192]{4,1,0,3,2:T(4,128)} %bitcast.5) | data formatting | bytes 8388608 | tf_op jit(solution)/shard_map/all_to_all | solution.py:98
  226.8 2.3 fusion.71
  229.1 3.1 reshape_squeeze.6
  232.2 4.8 %fusion.8 = f32[4,8,128,128]{3,2,1,0:T(8,128)} fusion(f32[4,8,128,128]{3,2,1,0:T(8,128)S(1)} %reshape_squeeze.6), kind=kOutput, calls=%fused_computation.107 | convolution fusion | flops 805535744 | bytes 4194304 | tf_op jit(solution)/shard_map/...ab,af->...bf/dot_general | solution.py:63
  237.0 3.5 reshape_squeeze.7
  240.5 1.3 copy-done.5
  241.8 3.6 fusion.6
  245.5 5.3 %convolution_add_fusion = f32[4,8,128,128]{3,2,1,0:T(8,128)S(1)} fusion(f32[4,8,128,128]{3,2,1,0:T(8,128)S(1)} %copy-done.6, f32[4,8,128,128]{3,2,1,0:T(8,128)} %copy-done.5), kind=kOutput, calls=%fused_computation.14 | convolution fusion | flops 806060032 | bytes 6291456 | tf_op jit(solution)/shard_map/...ab,af->...bf/dot_general | solution.py:63
  250.8 3.6 convolution_subtract_fusion
  254.4 2.5 fusion.1
  256.9 3.6 fusion
  260.5 3.7 subtract_bitcast_fusion
  264.2 2.7 stack.19
  266.9 4.3 %copy.89 = f32[1,1,4,8,16,1024]{5,3,2,4,0,1:T(8,128)} copy(f32[1,1,4,8,16,1024]{5,4,3,2,1,0:T(8,128)} %stack.19) | data formatting | bytes 4194304 | tf_op jit(solution)/shard_map/stack | solution.py:80
  271.2 3.7 add_bitcast_fusion
  274.9 1.9 stack.18
  278.4 1.4 maximum_multiply_fusion
  280.3 2.5 collective-permute-start.2
  282.8 2.6 collective-permute-start.3
  285.5 2.2 collective-permute-start.5
  288.3 2.2 collective-permute-done.2
  290.6 13.5 %collective-permute-done.3 = f32[1,2,1,4,8,1024]{5,4,3,0,1,2:T(8,128)S(1)} collective-permute-done((f32[1,2,1,4,8,1024]{5,4,3,0,1,2:T(8,128)S(1)}, f32[1,2,1,4,8,1024]{5,4,3,0,1,2:T(8,128)S(1)}, u32[]{:S(2)}, u32[]{:S(2)}) %collective-permute-start.3) | collective-permute-done | bytes 262176 | tf_op jit(solution)/shard_map/ppermute | solution.py:26
  305.0 1.4 collective-permute-start.9
  306.5 18.2 %collective-permute-start.10 = (f32[1,2,1,4,8,1024]{5,4,3,0,1,2:T(8,128)S(1)}, f32[1,2,1,4,8,1024]{5,4,3,0,1,2:T(8,128)S(1)}, u32[]{:S(2)}, u32[]{:S(2)}) collective-permute-start(f32[1,2,1,4,8,1024]{5,4,3,0,1,2:T(8,128)S(1)} %get-tuple-element.77), channel_id=1, source_target_pairs={{0,17},{1,18},{2,19},{3,24},{8,25},{9,26},{10,27},{11,0},{16,1},{1... | collective-permute-start | bytes 786440 | tf_op jit(solution)/shard_map/ppermute | solution.py:26
  324.8 11.9 %collective-permute-done.7 = f32[1,2,1,4,8,1024]{5,4,3,0,1,2:T(8,128)S(1)} collective-permute-done((f32[1,2,1,4,8,1024]{5,4,3,0,1,2:T(8,128)S(1)}, f32[1,2,1,4,8,1024]{5,4,3,0,1,2:T(8,128)S(1)}, u32[]{:S(2)}, u32[]{:S(2)}) %collective-permute-start.7) | collective-permute-done | bytes 262176 | tf_op jit(solution)/shard_map/ppermute | solution.py:26
  338.0 6.1 %collective-permute-start.14 = (f32[1,2,1,4,8,1024]{5,4,3,0,1,2:T(8,128)S(1)}, f32[1,2,1,4,8,1024]{5,4,3,0,1,2:T(8,128)S(1)}, u32[]{:S(2)}, u32[]{:S(2)}) collective-permute-start(f32[1,2,1,4,8,1024]{5,4,3,0,1,2:T(8,128)S(1)} %get-tuple-element.73), channel_id=1, source_target_pairs={{0,25},{1,26},{2,27},{3,0},{8,1},{9,2},{10,3},{11,8},{16,9},{17,10... | collective-permute-start | bytes 786440 | tf_op jit(solution)/shard_map/ppermute | solution.py:26
  344.2 15.2 %collective-permute-done.11 = f32[1,2,1,4,8,1024]{5,4,3,0,1,2:T(8,128)S(1)} collective-permute-done((f32[1,2,1,4,8,1024]{5,4,3,0,1,2:T(8,128)S(1)}, f32[1,2,1,4,8,1024]{5,4,3,0,1,2:T(8,128)S(1)}, u32[]{:S(2)}, u32[]{:S(2)}) %collective-permute-start.11) | collective-permute-done | bytes 262176 | tf_op jit(solution)/shard_map/ppermute | solution.py:26
  359.5 11.1 %collective-permute-done.15 = f32[1,2,1,4,8,1024]{5,4,3,0,1,2:T(8,128)S(1)} collective-permute-done((f32[1,2,1,4,8,1024]{5,4,3,0,1,2:T(8,128)S(1)}, f32[1,2,1,4,8,1024]{5,4,3,0,1,2:T(8,128)S(1)}, u32[]{:S(2)}, u32[]{:S(2)}) %collective-permute-start.15) | collective-permute-done | bytes 262176 | tf_op jit(solution)/shard_map/ppermute | solution.py:26
  370.6 2.3 collective-permute-done.16
  374.6 5.2 %multiply_add_fusion = f32[1,16,4,8,1024]{4,3,2,1,0:T(8,128)S(1)} fusion(f32[4,8,1024]{2,1,0:T(8,128)S(1)} %get-tuple-element.40, f32[16,1024]{1,0:T(8,128)S(1)} %get-tuple-element.126, f32[4,8,1024]{2,1,0:T(8,128)S(1)} %get-tuple-element.41, f32[16,1024]{1,0:T(8,128)S(1)} %get-tuple-element.127, f32[4,8,1024]{2,1,0:T(8,128)S(1)} %get-tuple-element.42, ...), kind=kLoop, calls=%fused_computation.4 | loop fusion | flops 33030144 | bytes 8388608 | tf_op jit(solution)/shard_map/add | solution.py:124
  379.8 5.3 %multiply_subtract_fusion = f32[1,16,4,8,1024]{4,3,2,1,0:T(8,128)S(1)} fusion(f32[4,8,1024]{2,1,0:T(8,128)S(1)} %get-tuple-element.40, f32[16,1024]{1,0:T(8,128)S(1)} %get-tuple-element.126, f32[4,8,1024]{2,1,0:T(8,128)S(1)} %get-tuple-element.41, f32[16,1024]{1,0:T(8,128)S(1)} %get-tuple-element.127, f32[4,8,1024]{2,1,0:T(8,128)S(1)} %get-tuple-element.42, ...), kind=kLoop, calls=%fused_computation.5 | loop fusion | flops 33030144 | bytes 8388608 | tf_op jit(solution)/shard_map/sub | solution.py:123
  385.1 2.3 pad_maximum_fusion.1
  (111 shorter events, 12.0 us)
Async XLA Ops:
  6.5 12.5 %copy-start.9 = (f32[2,17,16]{1,2,0:T(8,128)S(1)}, f32[2,17,16]{1,2,0:T(8,128)}, u32[]{:S(2)}) copy-start(f32[2,17,16]{1,2,0:T(8,128)} %param.5) | copy-start | bytes 6532
  6.5 168.1 %all-gather.2.cloned.1.call-start = ((), (), s32[]{:S(2)}) async-start(), calls=%async_computation.1 | async-start | bytes 3145728 | tf_op jit(solution)/shard_map/all_gather | solution.py:113
  11.2 50.1 %collective-permute-start = (f32[2,4,8,8192]{3,2,1,0:T(8,128)}, f32[2,4,8,8192]{3,2,1,0:T(8,128)}, u32[]{:S(2)}, u32[]{:S(2)}) collective-permute-start(f32[2,4,8,8192]{3,2,1,0:T(8,128)} %get-tuple-element.92), channel_id=1, source_target_pairs={{0,1},{1,2},{2,3},{4,5},{5,6},{6,7},{8,9},{9,10},{10,11},{12,13},{... | collective-permute-start | bytes 6291464 | tf_op jit(solution)/shard_map/ppermute | solution.py:38
  17.5 51.1 %collective-permute-start.1 = (f32[2,4,8,8192]{3,2,1,0:T(8,128)}, f32[2,4,8,8192]{3,2,1,0:T(8,128)}, u32[]{:S(2)}, u32[]{:S(2)}) collective-permute-start(f32[2,4,8,8192]{3,2,1,0:T(8,128)} %get-tuple-element.93), channel_id=1, source_target_pairs={{1,0},{2,1},{3,2},{5,4},{6,5},{7,6},{9,8},{10,9},{11,10},{13,12},{... | collective-permute-start | bytes 6291464 | tf_op jit(solution)/shard_map/ppermute | solution.py:39
  21.1 43.3 %copy-start = (f32[2,4,16,8192]{3,2,1,0:T(8,128)S(1)}, f32[2,4,16,8192]{3,2,1,0:T(8,128)}, u32[]{:S(2)}) copy-start(f32[2,4,16,8192]{3,2,1,0:T(8,128)} %param.4) | copy-start | bytes 12582916
  168.6 6.0 %copy-start.23 = (s32[16]{0:T(128)S(1)}, s32[16]{0:T(128)}, u32[]{:S(2)}) copy-start(s32[16]{0:T(128)} %param.7) | copy-start | bytes 196
  168.6 52.8 %all-to-all-start = ((f32[2,4,16,8192]{3,1,0,2:T(4,128)}), f32[2,4,16,8192]{3,1,0,2:T(4,128)}, u32[]{:S(2)}, u32[]{:S(2)}) async-start(f32[2,4,16,8192]{3,1,0,2:T(4,128)} %copy.76), calls=%async_computation | async-start | bytes 8388608 | tf_op jit(solution)/shard_map/all_to_all | solution.py:98
  232.2 4.9 %copy-start.3 = (f32[4,8,128,128]{3,2,1,0:T(8,128)}, f32[4,8,128,128]{3,2,1,0:T(8,128)S(1)}, u32[]{:S(2)}) copy-start(f32[4,8,128,128]{3,2,1,0:T(8,128)S(1)} %reshape_squeeze.6) | copy-start | bytes 6291460
  240.5 1.3 copy-start.5
  241.8 3.6 copy-start.6
  245.5 5.3 %copy-start.4 = (f32[4,8,128,128]{3,2,1,0:T(8,128)S(1)}, f32[4,8,128,128]{3,2,1,0:T(8,128)}, u32[]{:S(2)}) copy-start(f32[4,8,128,128]{3,2,1,0:T(8,128)} %copy-done.3) | copy-start | bytes 6291460
  254.4 6.1 %copy-start.1 = (f32[4,8,128,128]{3,2,1,0:T(8,128)}, f32[4,8,128,128]{3,2,1,0:T(8,128)S(1)}, u32[]{:S(2)}) copy-start(f32[4,8,128,128]{3,2,1,0:T(8,128)S(1)} %convolution_subtract_fusion) | copy-start | bytes 6291460
  266.9 4.3 %copy-start.2 = (f32[4,8,128,128]{3,2,1,0:T(8,128)S(1)}, f32[4,8,128,128]{3,2,1,0:T(8,128)}, u32[]{:S(2)}) copy-start(f32[4,8,128,128]{3,2,1,0:T(8,128)} %copy-done.1) | copy-start | bytes 6291460
  266.9 4.3 %copy-start.7 = (f32[128,4,8,128]{3,0,2,1:T(8,128)S(1)}, f32[128,4,8,128]{3,0,2,1:T(8,128)}, u32[]{:S(2)}) copy-start(f32[128,4,8,128]{3,0,2,1:T(8,128)} %fusion) | copy-start | bytes 6291460
  276.8 1.6 copy-start.8
  279.9 3.0 copy-start.21
  279.9 3.0 copy-start.22
  279.9 5.6 %copy-start.19 = (f32[1,16,1,1024]{3,2,1,0:T(1,128)S(1)}, f32[1,16,1,1024]{3,2,1,0:T(1,128)}, u32[]{:S(2)}) copy-start(f32[1,16,1,1024]{3,2,1,0:T(1,128)} %get-tuple-element.94) | copy-start | bytes 196612
  279.9 5.6 %copy-start.20 = (f32[1,16,1,1024]{3,2,1,0:T(1,128)S(1)}, f32[1,16,1,1024]{3,2,1,0:T(1,128)}, u32[]{:S(2)}) copy-start(f32[1,16,1,1024]{3,2,1,0:T(1,128)} %get-tuple-element.113) | copy-start | bytes 196612
  280.3 10.3 %collective-permute-start.2 = (f32[1,2,1,4,8,1024]{5,4,3,0,1,2:T(8,128)S(1)}, f32[1,2,1,4,8,1024]{5,4,3,0,1,2:T(8,128)S(1)}, u32[]{:S(2)}, u32[]{:S(2)}) collective-permute-start(f32[1,2,1,4,8,1024]{5,4,3,0,1,2:T(8,128)S(1)} %get-tuple-element.85), channel_id=1, source_target_pairs={{0,1},{1,2},{2,3},{3,8},{8,9},{9,10},{10,11},{11,16},{16,17},{17,1... | collective-permute-start | bytes 786440 | tf_op jit(solution)/shard_map/ppermute | solution.py:26
  282.8 21.3 %collective-permute-start.3 = (f32[1,2,1,4,8,1024]{5,4,3,0,1,2:T(8,128)S(1)}, f32[1,2,1,4,8,1024]{5,4,3,0,1,2:T(8,128)S(1)}, u32[]{:S(2)}, u32[]{:S(2)}) collective-permute-start(f32[1,2,1,4,8,1024]{5,4,3,0,1,2:T(8,128)S(1)} %get-tuple-element.84), channel_id=1, source_target_pairs={{0,2},{1,3},{2,8},{3,9},{8,10},{9,11},{10,16},{11,17},{16,18},{17,... | collective-permute-start | bytes 786440 | tf_op jit(solution)/shard_map/ppermute | solution.py:26
  285.5 19.5 %collective-permute-start.4 = (f32[1,2,1,4,8,1024]{5,4,3,0,1,2:T(8,128)S(1)}, f32[1,2,1,4,8,1024]{5,4,3,0,1,2:T(8,128)S(1)}, u32[]{:S(2)}, u32[]{:S(2)}) collective-permute-start(f32[1,2,1,4,8,1024]{5,4,3,0,1,2:T(8,128)S(1)} %get-tuple-element.83), channel_id=1, source_target_pairs={{0,3},{1,8},{2,9},{3,10},{8,11},{9,16},{10,17},{11,18},{16,19},{17... | collective-permute-start | bytes 786440 | tf_op jit(solution)/shard_map/ppermute | solution.py:26
  285.5 20.9 %collective-permute-start.5 = (f32[1,2,1,4,8,1024]{5,4,3,0,1,2:T(8,128)S(1)}, f32[1,2,1,4,8,1024]{5,4,3,0,1,2:T(8,128)S(1)}, u32[]{:S(2)}, u32[]{:S(2)}) collective-permute-start(f32[1,2,1,4,8,1024]{5,4,3,0,1,2:T(8,128)S(1)} %get-tuple-element.82), channel_id=1, source_target_pairs={{0,8},{1,9},{2,10},{3,11},{8,16},{9,17},{10,18},{11,19},{16,24},{1... | collective-permute-start | bytes 786440 | tf_op jit(solution)/shard_map/ppermute | solution.py:26
  287.7 37.0 %collective-permute-start.6 = (f32[1,2,1,4,8,1024]{5,4,3,0,1,2:T(8,128)S(1)}, f32[1,2,1,4,8,1024]{5,4,3,0,1,2:T(8,128)S(1)}, u32[]{:S(2)}, u32[]{:S(2)}) collective-permute-start(f32[1,2,1,4,8,1024]{5,4,3,0,1,2:T(8,128)S(1)} %get-tuple-element.81), channel_id=1, source_target_pairs={{0,9},{1,10},{2,11},{3,16},{8,17},{9,18},{10,19},{11,24},{16,25},{... | collective-permute-start | bytes 786440 | tf_op jit(solution)/shard_map/ppermute | solution.py:26
  290.5 46.2 %collective-permute-start.7 = (f32[1,2,1,4,8,1024]{5,4,3,0,1,2:T(8,128)S(1)}, f32[1,2,1,4,8,1024]{5,4,3,0,1,2:T(8,128)S(1)}, u32[]{:S(2)}, u32[]{:S(2)}) collective-permute-start(f32[1,2,1,4,8,1024]{5,4,3,0,1,2:T(8,128)S(1)} %get-tuple-element.80), channel_id=1, source_target_pairs={{0,10},{1,11},{2,16},{3,17},{8,18},{9,19},{10,24},{11,25},{16,26},... | collective-permute-start | bytes 786440 | tf_op jit(solution)/shard_map/ppermute | solution.py:26
  304.1 32.6 %collective-permute-start.8 = (f32[1,2,1,4,8,1024]{5,4,3,0,1,2:T(8,128)S(1)}, f32[1,2,1,4,8,1024]{5,4,3,0,1,2:T(8,128)S(1)}, u32[]{:S(2)}, u32[]{:S(2)}) collective-permute-start(f32[1,2,1,4,8,1024]{5,4,3,0,1,2:T(8,128)S(1)} %get-tuple-element.79), channel_id=1, source_target_pairs={{0,11},{1,16},{2,17},{3,18},{8,19},{9,24},{10,25},{11,26},{16,27},... | collective-permute-start | bytes 786440 | tf_op jit(solution)/shard_map/ppermute | solution.py:26
  305.0 32.9 %collective-permute-start.9 = (f32[1,2,1,4,8,1024]{5,4,3,0,1,2:T(8,128)S(1)}, f32[1,2,1,4,8,1024]{5,4,3,0,1,2:T(8,128)S(1)}, u32[]{:S(2)}, u32[]{:S(2)}) collective-permute-start(f32[1,2,1,4,8,1024]{5,4,3,0,1,2:T(8,128)S(1)} %get-tuple-element.78), channel_id=1, source_target_pairs={{0,16},{1,17},{2,18},{3,19},{8,24},{9,25},{10,26},{11,27},{16,0},{... | collective-permute-start | bytes 786440 | tf_op jit(solution)/shard_map/ppermute | solution.py:26
  306.5 37.6 %collective-permute-start.10 = (f32[1,2,1,4,8,1024]{5,4,3,0,1,2:T(8,128)S(1)}, f32[1,2,1,4,8,1024]{5,4,3,0,1,2:T(8,128)S(1)}, u32[]{:S(2)}, u32[]{:S(2)}) collective-permute-start(f32[1,2,1,4,8,1024]{5,4,3,0,1,2:T(8,128)S(1)} %get-tuple-element.77), channel_id=1, source_target_pairs={{0,17},{1,18},{2,19},{3,24},{8,25},{9,26},{10,27},{11,0},{16,1},{1... | collective-permute-start | bytes 786440 | tf_op jit(solution)/shard_map/ppermute | solution.py:26
  324.7 34.7 %collective-permute-start.11 = (f32[1,2,1,4,8,1024]{5,4,3,0,1,2:T(8,128)S(1)}, f32[1,2,1,4,8,1024]{5,4,3,0,1,2:T(8,128)S(1)}, u32[]{:S(2)}, u32[]{:S(2)}) collective-permute-start(f32[1,2,1,4,8,1024]{5,4,3,0,1,2:T(8,128)S(1)} %get-tuple-element.76), channel_id=1, source_target_pairs={{0,18},{1,19},{2,24},{3,25},{8,26},{9,27},{10,0},{11,1},{16,2},{17... | collective-permute-start | bytes 786440 | tf_op jit(solution)/shard_map/ppermute | solution.py:26
  336.7 22.7 %collective-permute-start.12 = (f32[1,2,1,4,8,1024]{5,4,3,0,1,2:T(8,128)S(1)}, f32[1,2,1,4,8,1024]{5,4,3,0,1,2:T(8,128)S(1)}, u32[]{:S(2)}, u32[]{:S(2)}) collective-permute-start(f32[1,2,1,4,8,1024]{5,4,3,0,1,2:T(8,128)S(1)} %get-tuple-element.75), channel_id=1, source_target_pairs={{0,19},{1,24},{2,25},{3,26},{8,27},{9,0},{10,1},{11,2},{16,3},{17,... | collective-permute-start | bytes 786440 | tf_op jit(solution)/shard_map/ppermute | solution.py:26
  336.8 22.7 %collective-permute-start.13 = (f32[1,2,1,4,8,1024]{5,4,3,0,1,2:T(8,128)S(1)}, f32[1,2,1,4,8,1024]{5,4,3,0,1,2:T(8,128)S(1)}, u32[]{:S(2)}, u32[]{:S(2)}) collective-permute-start(f32[1,2,1,4,8,1024]{5,4,3,0,1,2:T(8,128)S(1)} %get-tuple-element.74), channel_id=1, source_target_pairs={{0,24},{1,25},{2,26},{3,27},{8,0},{9,1},{10,2},{11,3},{16,8},{17,9... | collective-permute-start | bytes 786440 | tf_op jit(solution)/shard_map/ppermute | solution.py:26
  338.0 21.5 %collective-permute-start.14 = (f32[1,2,1,4,8,1024]{5,4,3,0,1,2:T(8,128)S(1)}, f32[1,2,1,4,8,1024]{5,4,3,0,1,2:T(8,128)S(1)}, u32[]{:S(2)}, u32[]{:S(2)}) collective-permute-start(f32[1,2,1,4,8,1024]{5,4,3,0,1,2:T(8,128)S(1)} %get-tuple-element.73), channel_id=1, source_target_pairs={{0,25},{1,26},{2,27},{3,0},{8,1},{9,2},{10,3},{11,8},{16,9},{17,10... | collective-permute-start | bytes 786440 | tf_op jit(solution)/shard_map/ppermute | solution.py:26
  344.1 26.5 %collective-permute-start.15 = (f32[1,2,1,4,8,1024]{5,4,3,0,1,2:T(8,128)S(1)}, f32[1,2,1,4,8,1024]{5,4,3,0,1,2:T(8,128)S(1)}, u32[]{:S(2)}, u32[]{:S(2)}) collective-permute-start(f32[1,2,1,4,8,1024]{5,4,3,0,1,2:T(8,128)S(1)} %get-tuple-element.72), channel_id=1, source_target_pairs={{0,26},{1,27},{2,0},{3,1},{8,2},{9,3},{10,8},{11,9},{16,10},{17,11... | collective-permute-start | bytes 786440 | tf_op jit(solution)/shard_map/ppermute | solution.py:26
  359.4 13.6 %collective-permute-start.16 = (f32[1,2,1,4,8,1024]{5,4,3,0,1,2:T(8,128)S(1)}, f32[1,2,1,4,8,1024]{5,4,3,0,1,2:T(8,128)S(1)}, u32[]{:S(2)}, u32[]{:S(2)}) collective-permute-start(f32[1,2,1,4,8,1024]{5,4,3,0,1,2:T(8,128)S(1)} %get-tuple-element.71), channel_id=1, source_target_pairs={{0,27},{1,0},{2,1},{3,2},{8,3},{9,8},{10,9},{11,10},{16,11},{17,16... | collective-permute-start | bytes 786440 | tf_op jit(solution)/shard_map/ppermute | solution.py:26
  373.5 0.8 copy-start.10
  373.5 0.9 copy-start.11
  373.5 0.9 copy-start.12
  373.5 0.9 copy-start.13
  373.5 0.9 copy-start.14
  373.5 1.0 copy-start.15
  373.5 1.0 copy-start.16
  373.5 1.0 copy-start.17
  373.5 1.0 copy-start.18
Sparse Core Ops, SparseCore 0:
  18.9 35.4 all-gather.1
